TPU v7x, 256 devices: a whole 4x4x8 slice. The times are simulated.
256 devices in a mesh: slab: 64 (over z, x, core), view: 4 (over y).
Axes of the slice: x: 4, y: 4, z: 8, core: 2. Of those that a mesh axis runs over, the one named last changes fastest.
Arguments:
- activity: float32 [2048, 32, 1024], P('slab'), may hold values from 0.5 to 2
- sensitivity: float32 [2048, 32, 1024], P('slab'), may hold values from 1 to 8
- psf_width: float32 [2048], P('slab'), may hold values from 0.05 to 0.3
- measured: bfloat16 [4, 4096, 32, 128], P('view', 'slab'), may hold values from 0.25 to 4
- block_slab: int32 [4, 4096, 1], P('view', 'slab'), may hold values from 0 to 63; in each aligned block of 64 rows (0 to 63, 64 to 127, ..., all dimensions but the last counted through in order) at most 2 rows name the same one
- block_line: int32 [4, 4096], P('view', 'slab'), may hold values from 0 to 31
- block_angle: int32 [4, 4096], P('view', 'slab'), may hold values from 0 to 7
- subset_views: int32 [4, 8], P('view'), may hold values from 0 to 335
Outputs:
- updated: float32 [2048, 32, 1024], P('slab')
Inputs may be any that keep to these rules, and one draw needn't show every extreme that they name: `block_slab`: among the 64 blocks of one device (aligned blocks of 64 rows) no slab is named more than 2 times, a bound that some block reaches.
All inputs are finite; a program needn't handle non-finite values.
Results may differ from a plain program's by a relative error of at most 0.0014.
Values may be sent and summed in bfloat16 or wider, within the bound.
A program may use at most 64 MiB of HBM per device.

v0:
```python
import math
import jax
import jax.numpy as jnp
from jax import lax
from jax.sharding import PartitionSpec as P

VIEWS_ALL = 336
BACKGROUND = 0.05


def with_halo(value, sides, width):
    for axis, dim in sides:
        size, length = (lax.axis_size(axis), value.shape[dim])
        up = [(i, (i + 1) % size) for i in range(size - 1)]
        down = [(j, i) for i, j in up]
        last = lax.slice_in_dim(value, length - width, length, axis=dim)
        leading = lax.slice_in_dim(value, 0, width, axis=dim)
        before = lax.ppermute(last, axis, up)
        after = lax.ppermute(leading, axis, down)
        value = jnp.concatenate([before, value, after], axis=dim)
    return value


def kernels(angles, bins, length):
    view_angle = math.pi * angles.astype(jnp.float32) / VIEWS_ALL
    step_width = length / bins
    deviation = 0.25 * step_width
    spacing = step_width * (0.75 + 0.25 * jnp.cos(2.0 * view_angle))
    offset = 1.5 * step_width * jnp.sin(view_angle)
    centres = (jnp.arange(bins, dtype=jnp.float32) + 0.5 - bins / 2)[None, :] * spacing[
        :, None
    ] + offset[:, None]
    voxel_pos = jnp.arange(length, dtype=jnp.float32) + 0.5 - length / 2
    distance = voxel_pos[None, None, :] - centres[:, :, None]
    values = jnp.exp(-distance * distance / (2.0 * deviation * deviation)) / (
        deviation * math.sqrt(2.0 * math.pi)
    )
    return values.astype(jnp.bfloat16)


def on_device(
    activity, sensitivity, psf_width, measured, block_slab, block_line, block_angle, subset_views
):
    weight = psf_width[:, None, None]
    padded = with_halo(activity, (("slab", 0),), 1)
    blurred = ((1.0 - 2.0 * weight) * activity + weight * (padded[:-2] + padded[2:])).astype(
        jnp.bfloat16
    )
    planes, lines_here, length = activity.shape
    bins = measured.shape[3]
    tof_kernel = kernels(subset_views[0], bins, length)
    angle_count = tof_kernel.shape[0]
    projected = jnp.einsum("zlv,atv->alzt", blurred, tof_kernel, preferred_element_type=jnp.float32)
    projected = projected.reshape(angle_count * lines_here, planes, bins)
    slab_count = lax.axis_size("slab")
    block_total = measured.shape[1]
    capacity = 2 * block_total // slab_count
    targets = block_slab[0, :, 0]
    onehot = (targets[:, None] == jnp.arange(slab_count, dtype=jnp.int32)[None, :]).astype(
        jnp.int32
    )
    slot_pos = jnp.sum((jnp.cumsum(onehot, axis=0) - onehot) * onehot, axis=1)
    send_rows = (
        jnp.zeros((slab_count, capacity, planes, bins), jnp.bfloat16)
        .at[targets, slot_pos]
        .set(measured[0])
    )
    send_index = (
        jnp.zeros((slab_count, capacity), jnp.int32)
        .at[targets, slot_pos]
        .set(block_angle[0] * lines_here + block_line[0])
    )
    rows = lax.all_to_all(send_rows, "slab", split_axis=0, concat_axis=0, tiled=True)
    index = lax.all_to_all(send_index, "slab", split_axis=0, concat_axis=0, tiled=True)
    estimate = projected[index]
    ratios, index = (rows.astype(jnp.float32) / (estimate + BACKGROUND), index)
    sums = jnp.zeros((angle_count * lines_here, planes, bins), jnp.float32)
    sums = sums.at[index.reshape(-1)].add(ratios.reshape(-1, planes, bins))
    rounded = sums.astype(jnp.bfloat16).reshape(angle_count, lines_here, planes, bins)
    back = jnp.einsum("alzt,atv->zlv", rounded, tof_kernel, preferred_element_type=jnp.float32)
    total = lax.psum(back, "view")
    edges = with_halo(weight * total, (("slab", 0),), 1)
    smoothed = (1.0 - 2.0 * weight) * total + edges[:-2] + edges[2:]
    return activity * smoothed / sensitivity


def solution(mesh):
    in_specs = (
        P("slab", None, None),
        P("slab", None, None),
        P("slab"),
        P("view", "slab", None, None),
        P("view", "slab", None),
        P("view", "slab"),
        P("view", "slab"),
        P("view", None),
    )
    out_specs = P("slab", None, None)
    return jax.shard_map(
        on_device, mesh=mesh, in_specs=in_specs, out_specs=out_specs, check_vma=False
    )
```

profile of v0, /device:TPU:103, one launch (start us, length us, event | category | flops | bytes accessed | tf_op | source)
XLA Modules:
  0.0 249.0 jit_solution(8091599429287186392)
XLA Ops:
  6.5 0.7 fusion.23
  7.4 0.8 select_reduce_fusion
  8.9 0.7 add_bitcast_fusion
  9.6 3.5 %scatter_fusion = s32[64,2]{0,1:T(2,128)S(1)} fusion(s32[64,2]{0,1:T(2,128)S(1)} %broadcast.188, s32[64]{0:T(128)S(1)} %fusion.26, s32[64]{0:T(128)S(1)} %add_bitcast_fusion), kind=kCustom, calls=%fused_computation.1 | custom fusion | bytes 1280 | tf_op jit(solution)/shard_map/scatter | solution.py:71
  13.1 0.7 copy.33
  13.8 11.0 %all-to-all-start = ((s32[64,1,2]{2,1,0:T(1,128)}), s32[64,1,2]{2,1,0:T(1,128)S(1)}, u32[]{:S(2)}, u32[]{:S(2)}) async-start(s32[64,1,2]{2,1,0:T(1,128)} %copy.33), calls=%async_computation | async-start | bytes 65536 | tf_op jit(solution)/shard_map/all_to_all | solution.py:74
  24.8 1.0 fusion.32
  25.9 2.3 collective-permute-start.1
  28.3 6.6 %collective-permute-start = (f32[1,32,1024]{2,0,1:T(1,128)S(1)}, f32[1,32,1024]{2,0,1:T(1,128)S(1)}, u32[]{:S(2)}, u32[]{:S(2)}) collective-permute-start(f32[1,32,1024]{2,0,1:T(1,128)S(1)} %copy.35), channel_id=1, source_target_pairs={{0,4},{4,8},{8,12},{12,16},{16,20},{20,24},{24,28},{28,32},{32,36}... | collective-permute-start | bytes 393224 | tf_op jit(solution)/shard_map/ppermute | solution.py:18
  35.0 0.7 multiply_bitcast_fusion
  35.8 1.2 broadcast_in_dim.5
  37.0 8.0 %scatter_fusion.1 = bf16[64,2,32,128]{3,2,1,0:T(8,128)(2,1)} fusion(bf16[64,2,32,128]{3,2,1,0:T(8,128)(2,1)} %broadcast_in_dim.5, s32[64]{0:T(128)S(1)} %fusion.26, bf16[64,32,128]{2,1,0:T(8,128)(2,1)} %bitcast.57), kind=kCustom, calls=%fused_computation.2 | custom fusion | bytes 1573376 | tf_op jit(solution)/shard_map/scatter | solution.py:66
  45.0 8.6 %all-to-all-start.1 = ((bf16[64,2,32,128]{3,2,1,0:T(8,128)(2,1)}), bf16[64,2,32,128]{3,2,1,0:T(8,128)(2,1)S(1)}, u32[]{:S(2)}, u32[]{:S(2)}) async-start(bf16[64,2,32,128]{3,2,1,0:T(8,128)(2,1)} %scatter_fusion.1), calls=%async_computation.1 | async-start | bytes 2097152 | tf_op jit(solution)/shard_map/all_to_all | solution.py:73
  53.7 6.6 %copy.44 = f32[32,32,1024]{2,0,1:T(8,128)} copy(f32[32,32,1024]{2,1,0:T(8,128)} %param.8) | data formatting | bytes 8388608 | tf_op args[0]
  60.9 0.8 reduce.3
  62.2 6.8 %fusion.11 = bf16[32,32,1024]{2,0,1:T(8,128)(2,1)S(1)} fusion(f32[1,32,1024]{2,0,1:T(1,128)S(1)} %collective-permute-done.1, f32[32,32,1024]{2,0,1:T(8,128)} %copy.44, f32[1,32,1024]{2,0,1:T(1,128)S(1)} %collective-permute-done, f32[32]{0:T(128)S(1)} %copy-done.2, f32[32]{0:T(128)S(1)} %multiply_subtract_fusion), kind=kLoop, calls=%fused_computation.19 | loop fusion | flops 7340032 | bytes 6553856 | tf_op jit(solution)/shard_map/convert_element_type | solution.py:46
  69.0 3.3 %convolution_bitcast_fusion.1 = f32[8,32,32,128]{3,1,2,0:T(8,128)S(1)} fusion(bf16[32,32,1024]{2,0,1:T(8,128)(2,1)S(1)} %fusion.11, f32[8,128]{1,0:T(8,128)S(1)} %multiply_add_fusion, f32[1024]{0:T(1024)S(1)} %iota_add_fusion), kind=kOutput, calls=%fused_computation.22 | convolution fusion | flops 2153775104 | bytes 6299648 | tf_op jit(solution)/shard_map/zlv,atv->alzt/dot_general | solution.py:53
  72.3 4.4 %copy.40 = f32[8,32,32,128]{3,2,1,0:T(8,128)} copy(f32[8,32,32,128]{3,1,2,0:T(8,128)S(1)} %convolution_bitcast_fusion.1) | data formatting | bytes 8388608 | tf_op jit(solution)/shard_map/zlv,atv->alzt/transpose | solution.py:53
  76.7 2.9 %gather_fusion = f32[128,32,128]{2,1,0:T(8,128)S(1)} fusion(f32[256,32,128]{2,1,0:T(8,128)} %bitcast.53, s32[1024]{0:T(1024)S(1)} %pad_clamp_fusion), kind=kCustom, calls=%fused_computation | custom fusion | bytes 4194816 | tf_op jit(solution)/shard_map/gather | solution.py:75
  79.5 1.6 broadcast_add_fusion
  81.1 2.0 convert_divide_fusion
  83.1 2.5 %broadcast_in_dim.4 = f32[256,32,128]{2,1,0:T(8,128)} broadcast(f32[]{:T(128)} %constant.17.clone.1), dimensions={} | broadcast | bytes 4194308 | tf_op jit(solution)/shard_map/broadcast_in_dim | solution.py:77
  85.6 18.3 %scatter_fusion.2 = f32[256,32,128]{2,1,0:T(8,128)} fusion(f32[256,32,128]{2,1,0:T(8,128)} %broadcast_in_dim.4, s32[128]{0:T(128)S(1)} %fusion.25, f32[128,32,128]{2,1,0:T(8,128)S(1)} %bitcast.54), kind=kCustom, calls=%fused_computation.3 | custom fusion | flops 524288 | bytes 6291968 | tf_op jit(solution)/shard_map/scatter-add | solution.py:78
  103.9 2.7 %convert_element_type.31 = bf16[256,32,128]{2,1,0:T(8,128)(2,1)S(1)} convert(f32[256,32,128]{2,1,0:T(8,128)} %scatter_fusion.2) | non-fusion elementwise | flops 1048576 | bytes 6291456 | tf_op jit(solution)/shard_map/convert_element_type | solution.py:79
  106.6 4.6 %convolution_bitcast_fusion = f32[32,32,1024]{2,0,1:T(8,128)} fusion(bf16[8,32,32,128]{3,2,1,0:T(8,128)(2,1)S(1)} %bitcast.56, f32[8,128]{1,0:T(8,128)S(1)} %multiply_add_fusion, f32[1024]{0:T(1024)S(1)} %iota_add_fusion), kind=kOutput, calls=%fused_computation.21 | convolution fusion | flops 2153775104 | bytes 6299648 | tf_op jit(solution)/shard_map/alzt,atv->zlv/dot_general | solution.py:80
  111.2 99.1 %all-reduce.2.cloned.1.call-done = f32[32,32,1024]{2,0,1:T(8,128)} async-done(((f32[32,32,1024]{2,0,1:T(8,128)}), f32[32,32,1024]{2,0,1:T(8,128)}) %all-reduce.2.cloned.1.call-update) | async-done | bytes 4194320 | tf_op jit(solution)/shard_map/psum | solution.py:81
  210.3 3.1 %broadcast_multiply_fusion = f32[32,32,1024]{2,0,1:T(8,128)S(1)} fusion(f32[32,32,1024]{2,0,1:T(8,128)} %all-reduce.2.cloned.1.call-done, f32[32]{0:T(128)S(1)} %copy-done.2), kind=kLoop, calls=%fused_computation.26 | loop fusion | flops 1048576 | bytes 8388736 | tf_op jit(solution)/shard_map/mul | solution.py:82
  213.6 5.1 %collective-permute-start.2 = (f32[1,32,1024]{2,0,1:T(1,128)S(1)}, f32[1,32,1024]{2,0,1:T(1,128)S(1)}, u32[]{:S(2)}, u32[]{:S(2)}) collective-permute-start(f32[1,32,1024]{2,0,1:T(1,128)S(1)} %get-tuple-element.5), channel_id=1, source_target_pairs={{0,4},{4,8},{8,12},{12,16},{16,20},{20,24},{24,28},{28,32},{32,36}... | collective-permute-start | bytes 393224 | tf_op jit(solution)/shard_map/ppermute | solution.py:18
  218.7 1.9 collective-permute-start.3
  220.7 7.7 %collective-permute-done.3 = f32[1,32,1024]{2,0,1:T(1,128)S(1)} collective-permute-done((f32[1,32,1024]{2,0,1:T(1,128)S(1)}, f32[1,32,1024]{2,0,1:T(1,128)S(1)}, u32[]{:S(2)}, u32[]{:S(2)}) %collective-permute-start.3) | collective-permute-done | bytes 131104 | tf_op jit(solution)/shard_map/ppermute | solution.py:19
  228.3 9.4 %fusion.6 = f32[32,32,1024]{2,0,1:T(8,128)S(1)} fusion(f32[1,32,1024]{2,0,1:T(1,128)S(1)} %collective-permute-done.3, f32[32,32,1024]{2,0,1:T(8,128)S(1)} %broadcast_multiply_fusion, f32[1,32,1024]{2,0,1:T(1,128)S(1)} %collective-permute-done.2, f32[32,32,1024]{2,1,0:T(8,128)} %param.9, f32[32,32,1024]{2,0,1:T(8,128)S(1)} %copy-done.1, ...), kind=kLoop, calls=%fused_computation.12 | loop fusion | flops 7340032 | bytes 21233792 | tf_op jit(solution)/shard_map/div | solution.py:84
  237.7 4.4 %copy.46 = f32[32,32,1024]{2,1,0:T(8,128)} copy(f32[32,32,1024]{2,0,1:T(8,128)S(1)} %fusion.6) | data formatting | bytes 8388608 | tf_op jit(solution)/shard_map/div | solution.py:84
  (31 shorter events, 2.5 us)
Async XLA Ops:
  6.5 47.1 %copy-start.2 = (f32[32]{0:T(128)S(1)}, f32[32]{0:T(128)}, u32[]{:S(2)}) copy-start(f32[32]{0:T(128)} %param.10) | copy-start | bytes 388
  13.8 31.2 %all-to-all-start = ((s32[64,1,2]{2,1,0:T(1,128)}), s32[64,1,2]{2,1,0:T(1,128)S(1)}, u32[]{:S(2)}, u32[]{:S(2)}) async-start(s32[64,1,2]{2,1,0:T(1,128)} %copy.33), calls=%async_computation | async-start | bytes 65536 | tf_op jit(solution)/shard_map/all_to_all | solution.py:74
  25.9 36.2 %collective-permute-start.1 = (f32[1,32,1024]{2,0,1:T(1,128)S(1)}, f32[1,32,1024]{2,0,1:T(1,128)S(1)}, u32[]{:S(2)}, u32[]{:S(2)}) collective-permute-start(f32[1,32,1024]{2,0,1:T(1,128)S(1)} %copy.37), channel_id=1, source_target_pairs={{4,0},{8,4},{12,8},{16,12},{20,16},{24,20},{28,24},{32,28},{36,32}... | collective-permute-start | bytes 393224 | tf_op jit(solution)/shard_map/ppermute | solution.py:19
  28.3 33.8 %collective-permute-start = (f32[1,32,1024]{2,0,1:T(1,128)S(1)}, f32[1,32,1024]{2,0,1:T(1,128)S(1)}, u32[]{:S(2)}, u32[]{:S(2)}) collective-permute-start(f32[1,32,1024]{2,0,1:T(1,128)S(1)} %copy.35), channel_id=1, source_target_pairs={{0,4},{4,8},{8,12},{12,16},{16,20},{20,24},{24,28},{28,32},{32,36}... | collective-permute-start | bytes 393224 | tf_op jit(solution)/shard_map/ppermute | solution.py:18
  45.0 36.1 %all-to-all-start.1 = ((bf16[64,2,32,128]{3,2,1,0:T(8,128)(2,1)}), bf16[64,2,32,128]{3,2,1,0:T(8,128)(2,1)S(1)}, u32[]{:S(2)}, u32[]{:S(2)}) async-start(bf16[64,2,32,128]{3,2,1,0:T(8,128)(2,1)} %scatter_fusion.1), calls=%async_computation.1 | async-start | bytes 2097152 | tf_op jit(solution)/shard_map/all_to_all | solution.py:73
  53.6 156.8 %all-reduce.2.cloned.1.call-start = ((), (), s32[]{:S(2)}) async-start(), calls=%async_computation.2 | async-start | bytes 8388608 | tf_op jit(solution)/shard_map/psum | solution.py:81
  210.3 18.0 %copy-start = (f32[32,32,1024]{2,1,0:T(8,128)S(1)}, f32[32,32,1024]{2,1,0:T(8,128)}, u32[]{:S(2)}) copy-start(f32[32,32,1024]{2,1,0:T(8,128)} %param.8) | copy-start | bytes 12582916
  210.3 18.0 %copy-start.1 = (f32[32,32,1024]{2,0,1:T(8,128)S(1)}, f32[32,32,1024]{2,0,1:T(8,128)}, u32[]{:S(2)}) copy-start(f32[32,32,1024]{2,0,1:T(8,128)} %all-reduce.2.cloned.1.call-done) | copy-start | bytes 12582916
  213.6 7.0 %collective-permute-start.2 = (f32[1,32,1024]{2,0,1:T(1,128)S(1)}, f32[1,32,1024]{2,0,1:T(1,128)S(1)}, u32[]{:S(2)}, u32[]{:S(2)}) collective-permute-start(f32[1,32,1024]{2,0,1:T(1,128)S(1)} %get-tuple-element.5), channel_id=1, source_target_pairs={{0,4},{4,8},{8,12},{12,16},{16,20},{20,24},{24,28},{28,32},{32,36}... | collective-permute-start | bytes 393224 | tf_op jit(solution)/shard_map/ppermute | solution.py:18
  218.7 9.6 %collective-permute-start.3 = (f32[1,32,1024]{2,0,1:T(1,128)S(1)}, f32[1,32,1024]{2,0,1:T(1,128)S(1)}, u32[]{:S(2)}, u32[]{:S(2)}) collective-permute-start(f32[1,32,1024]{2,0,1:T(1,128)S(1)} %get-tuple-element.6), channel_id=1, source_target_pairs={{4,0},{8,4},{12,8},{16,12},{20,16},{24,20},{28,24},{32,28},{36,32}... | collective-permute-start | bytes 393224 | tf_op jit(solution)/shard_map/ppermute | solution.py:19
Sparse Core Ops, SparseCore 0:
  111.3 98.9 all-reduce.1
where the time goes:
time: 250 us; the launch traced here: 249 us
  waiting for transfers between devices  107 us (43%)
  other arithmetic  48.3 us (19%)
  local copies, waits for them, and re-layouts  36.9 us (15%)
  starting transfers between devices  35.5 us (14%)
  between operations  13.6 us (5%)
  matrix products  7.89 us (3%)
    psum x1, waiting for transfers between devices, on_device(): total = lax.psum(back, 'view')  99.1 us
    scatter-add x1, other arithmetic, on_device(): sums = sums.at[index.reshape(-1)].add(ratios.reshape(-1, planes, bins))  18.3 us
    ppermute x2, starting transfers between devices, with_halo(): before = lax.ppermute(last, axis, up)  11.7 us
    all_to_all x1, starting transfers between devices, on_device(): lax.all_to_all(send_index, 'slab', split_axis=0, concat_axis=0, tiled=True)  11 us
    div x1, other arithmetic, on_device(): return activity * smoothed / sensitivity  9.36 us
    all_to_all x1, starting transfers between devices, on_device(): lax.all_to_all(send_rows, 'slab', split_axis=0, concat_axis=0, tiled=True)  8.57 us
    scatter x1, local copies, waits for them, and re-layouts, on_device(): send_rows = jnp.zeros((slab_count, capacity, planes, bins), jnp.bfloat16)...  8 us
    ppermute x2, waiting for transfers between devices, with_halo(): after = lax.ppermute(leading, axis, down)  7.67 us
  transfers between devices with their start and end apart: 7, of which 2 were waited for; matrix products, arithmetic and copies ran while one was open for 16% of the time, Pallas kernels for 0%

commit v1 on v0

--- a/solution.py
+++ b/solution.py
@@ -78,7 +78,8 @@
     sums = sums.at[index.reshape(-1)].add(ratios.reshape(-1, planes, bins))
     rounded = sums.astype(jnp.bfloat16).reshape(angle_count, lines_here, planes, bins)
     back = jnp.einsum("alzt,atv->zlv", rounded, tof_kernel, preferred_element_type=jnp.float32)
-    total = lax.psum(back, "view")
+    tall = lax.all_gather(back, axis_name="view")
+    total = jnp.sum(tall, 0)
     edges = with_halo(weight * total, (("slab", 0),), 1)
     smoothed = (1.0 - 2.0 * weight) * total + edges[:-2] + edges[2:]
     return activity * smoothed / sensitivity

time: 250 us -> 318 us (1.27)
  waiting for transfers between devices: 107 us -> 165 us
  other arithmetic: 48.3 us -> 57.4 us
    all_gather x0 -> x1, waiting for transfers between devices: none -> 158 us  [on_device(): tall = lax.all_gather(back, axis_name='view')]
    psum x1 -> x0, waiting for transfers between devices: 99.1 us -> none  [on_device(): total = lax.psum(back, 'view')]
    reduce_sum x0 -> x1, other arithmetic: none -> 10.4 us  [on_device(): total = jnp.sum(tall, 0)]
  transfers between devices with their start and end apart: 7 -> 7, of which waited for: 2 -> 2; matrix products, arithmetic and copies ran while one was open for 16% -> 12% of each run, Pallas kernels for 0% -> 0%
where the time goes in v1:
time: 318 us; the launch traced here: 317 us
  waiting for transfers between devices  165 us (52%)
  other arithmetic  57.4 us (18%)
  local copies, waits for them, and re-layouts  36.9 us (12%)
  starting transfers between devices  35.5 us (11%)
  between operations  13.6 us (4%)
  matrix products  7.87 us (2%)
    all_gather x1, waiting for transfers between devices, on_device(): tall = lax.all_gather(back, axis_name='view')  158 us
    scatter-add x1, other arithmetic, on_device(): sums = sums.at[index.reshape(-1)].add(ratios.reshape(-1, planes, bins))  16.9 us
    ppermute x2, starting transfers between devices, with_halo(): before = lax.ppermute(last, axis, up)  11.7 us
    all_to_all x1, starting transfers between devices, on_device(): lax.all_to_all(send_index, 'slab', split_axis=0, concat_axis=0, tiled=True)  11 us
    reduce_sum x1, other arithmetic, on_device(): total = jnp.sum(tall, 0)  10.4 us
    div x1, other arithmetic, on_device(): return activity * smoothed / sensitivity  9.36 us
    all_to_all x1, starting transfers between devices, on_device(): lax.all_to_all(send_rows, 'slab', split_axis=0, concat_axis=0, tiled=True)  8.57 us
    scatter x1, local copies, waits for them, and re-layouts, on_device(): send_rows = jnp.zeros((slab_count, capacity, planes, bins), jnp.bfloat16)...  8 us
  transfers between devices with their start and end apart: 7, of which 2 were waited for; matrix products, arithmetic and copies ran while one was open for 12% of the time, Pallas kernels for 0%

profile of v1, /device:TPU:103, one launch (start us, length us, event | category | flops | bytes accessed | tf_op | source)
XLA Modules:
  0.0 316.5 jit_solution(8112238644249924897)
XLA Ops:
  6.5 0.7 fusion.23
  7.4 0.8 select_reduce_fusion
  9.6 3.5 %scatter_fusion = s32[64,2]{0,1:T(2,128)S(1)} fusion(s32[64,2]{0,1:T(2,128)S(1)} %broadcast.188, s32[64]{0:T(128)S(1)} %fusion.26, s32[64]{0:T(128)S(1)} %add_bitcast_fusion), kind=kCustom, calls=%fused_computation.1 | custom fusion | bytes 1280 | tf_op jit(solution)/shard_map/scatter | solution.py:71
  13.1 0.7 copy.15
  13.8 11.0 %all-to-all-start = ((s32[64,1,2]{2,1,0:T(1,128)}), s32[64,1,2]{2,1,0:T(1,128)S(1)}, u32[]{:S(2)}, u32[]{:S(2)}) async-start(s32[64,1,2]{2,1,0:T(1,128)} %copy.15), calls=%async_computation | async-start | bytes 65536 | tf_op jit(solution)/shard_map/all_to_all | solution.py:74
  24.8 1.0 fusion.32
  25.9 2.3 collective-permute-start.1
  28.3 6.6 %collective-permute-start = (f32[1,32,1024]{2,0,1:T(1,128)S(1)}, f32[1,32,1024]{2,0,1:T(1,128)S(1)}, u32[]{:S(2)}, u32[]{:S(2)}) collective-permute-start(f32[1,32,1024]{2,0,1:T(1,128)S(1)} %copy.17), channel_id=1, source_target_pairs={{0,4},{4,8},{8,12},{12,16},{16,20},{20,24},{24,28},{28,32},{32,36}... | collective-permute-start | bytes 393224 | tf_op jit(solution)/shard_map/ppermute | solution.py:18
  35.0 0.7 multiply_bitcast_fusion
  35.8 1.2 broadcast_in_dim.5
  37.0 8.0 %scatter_fusion.1 = bf16[64,2,32,128]{3,2,1,0:T(8,128)(2,1)} fusion(bf16[64,2,32,128]{3,2,1,0:T(8,128)(2,1)} %broadcast_in_dim.5, s32[64]{0:T(128)S(1)} %fusion.26, bf16[64,32,128]{2,1,0:T(8,128)(2,1)} %bitcast.59), kind=kCustom, calls=%fused_computation.2 | custom fusion | bytes 1573376 | tf_op jit(solution)/shard_map/scatter | solution.py:66
  45.0 8.6 %all-to-all-start.1 = ((bf16[64,2,32,128]{3,2,1,0:T(8,128)(2,1)}), bf16[64,2,32,128]{3,2,1,0:T(8,128)(2,1)S(1)}, u32[]{:S(2)}, u32[]{:S(2)}) async-start(bf16[64,2,32,128]{3,2,1,0:T(8,128)(2,1)} %scatter_fusion.1), calls=%async_computation.1 | async-start | bytes 2097152 | tf_op jit(solution)/shard_map/all_to_all | solution.py:73
  53.7 6.6 %copy.26 = f32[32,32,1024]{2,0,1:T(8,128)} copy(f32[32,32,1024]{2,1,0:T(8,128)} %param.8) | data formatting | bytes 8388608 | tf_op args[0]
  60.9 0.8 reduce.3
  62.2 6.8 %fusion.11 = bf16[32,32,1024]{2,0,1:T(8,128)(2,1)S(1)} fusion(f32[1,32,1024]{2,0,1:T(1,128)S(1)} %collective-permute-done.1, f32[32,32,1024]{2,0,1:T(8,128)} %copy.26, f32[1,32,1024]{2,0,1:T(1,128)S(1)} %collective-permute-done, f32[32]{0:T(128)S(1)} %copy-done.2, f32[32]{0:T(128)S(1)} %multiply_subtract_fusion), kind=kLoop, calls=%fused_computation.19 | loop fusion | flops 7340032 | bytes 6553856 | tf_op jit(solution)/shard_map/convert_element_type | solution.py:46
  69.0 3.3 %convolution_bitcast_fusion.1 = f32[8,32,32,128]{3,1,2,0:T(8,128)S(1)} fusion(bf16[32,32,1024]{2,0,1:T(8,128)(2,1)S(1)} %fusion.11, f32[8,128]{1,0:T(8,128)S(1)} %multiply_add_fusion, f32[1024]{0:T(1024)S(1)} %iota_add_fusion), kind=kOutput, calls=%fused_computation.22 | convolution fusion | flops 2153775104 | bytes 6299648 | tf_op jit(solution)/shard_map/zlv,atv->alzt/dot_general | solution.py:53
  72.3 4.4 %copy.22 = f32[8,32,32,128]{3,2,1,0:T(8,128)} copy(f32[8,32,32,128]{3,1,2,0:T(8,128)S(1)} %convolution_bitcast_fusion.1) | data formatting | bytes 8388608 | tf_op jit(solution)/shard_map/zlv,atv->alzt/transpose | solution.py:53
  76.7 2.9 gather_fusion
  79.6 1.6 broadcast_add_fusion
  81.1 2.0 convert_divide_fusion
  83.1 2.5 broadcast_in_dim.4
  85.7 16.9 %scatter_fusion.2 = f32[256,32,128]{2,1,0:T(8,128)} fusion(f32[256,32,128]{2,1,0:T(8,128)} %broadcast_in_dim.4, s32[128]{0:T(128)S(1)} %fusion.25, f32[128,32,128]{2,1,0:T(8,128)S(1)} %bitcast.56), kind=kCustom, calls=%fused_computation.3 | custom fusion | flops 524288 | bytes 6291968 | tf_op jit(solution)/shard_map/scatter-add | solution.py:78
  102.6 2.7 convert_element_type.31
  105.3 4.6 %convolution_bitcast_fusion = f32[32,32,1024]{2,0,1:T(8,128)} fusion(bf16[8,32,32,128]{3,2,1,0:T(8,128)(2,1)S(1)} %bitcast.58, f32[8,128]{1,0:T(8,128)S(1)} %multiply_add_fusion, f32[1024]{0:T(1024)S(1)} %iota_add_fusion), kind=kOutput, calls=%fused_computation.21 | convolution fusion | flops 2153775104 | bytes 6299648 | tf_op jit(solution)/shard_map/alzt,atv->zlv/dot_general | solution.py:80
  109.9 157.6 %all-gather.3.cloned.1.call-done = f32[128,32,1024]{2,0,1:T(8,128)} async-done(((f32[32,32,1024]{2,0,1:T(8,128)}), f32[128,32,1024]{2,0,1:T(8,128)}) %all-gather.3.cloned.1.call-update) | async-done | bytes 16777232 | tf_op jit(solution)/shard_map/all_gather | solution.py:81
  267.5 10.4 %reduce_sum.22 = f32[32,32,1024]{2,0,1:T(8,128)} reduce(f32[4,32,32,1024]{3,1,0,2:T(8,128)} %bitcast.54, f32[]{:T(128)} %constant.16.clone.1), dimensions={0}, to_apply=%region_5.6 | reduce | flops 3145728 | bytes 20971524 | tf_op jit(solution)/shard_map/reduce_sum | solution.py:82
  277.9 3.1 broadcast_multiply_fusion
  281.2 5.1 %collective-permute-start.2 = (f32[1,32,1024]{2,0,1:T(1,128)S(1)}, f32[1,32,1024]{2,0,1:T(1,128)S(1)}, u32[]{:S(2)}, u32[]{:S(2)}) collective-permute-start(f32[1,32,1024]{2,0,1:T(1,128)S(1)} %get-tuple-element.5), channel_id=1, source_target_pairs={{0,4},{4,8},{8,12},{12,16},{16,20},{20,24},{24,28},{28,32},{32,36}... | collective-permute-start | bytes 393224 | tf_op jit(solution)/shard_map/ppermute | solution.py:18
  286.3 1.9 collective-permute-start.3
  288.2 7.7 %collective-permute-done.3 = f32[1,32,1024]{2,0,1:T(1,128)S(1)} collective-permute-done((f32[1,32,1024]{2,0,1:T(1,128)S(1)}, f32[1,32,1024]{2,0,1:T(1,128)S(1)}, u32[]{:S(2)}, u32[]{:S(2)}) %collective-permute-start.3) | collective-permute-done | bytes 131104 | tf_op jit(solution)/shard_map/ppermute | solution.py:19
  295.9 9.4 %fusion.6 = f32[32,32,1024]{2,0,1:T(8,128)S(1)} fusion(f32[1,32,1024]{2,0,1:T(1,128)S(1)} %collective-permute-done.3, f32[32,32,1024]{2,0,1:T(8,128)S(1)} %broadcast_multiply_fusion, f32[1,32,1024]{2,0,1:T(1,128)S(1)} %collective-permute-done.2, f32[32,32,1024]{2,1,0:T(8,128)} %param.9, f32[32,32,1024]{2,0,1:T(8,128)S(1)} %copy-done, ...), kind=kLoop, calls=%fused_computation.12 | loop fusion | flops 7340032 | bytes 21233792 | tf_op jit(solution)/shard_map/div | solution.py:85
  305.2 4.4 %copy.28 = f32[32,32,1024]{2,1,0:T(8,128)} copy(f32[32,32,1024]{2,0,1:T(8,128)S(1)} %fusion.6) | data formatting | bytes 8388608 | tf_op jit(solution)/shard_map/div | solution.py:85
  (32 shorter events, 3.2 us)
Async XLA Ops:
  6.5 47.1 %copy-start.2 = (f32[32]{0:T(128)S(1)}, f32[32]{0:T(128)}, u32[]{:S(2)}) copy-start(f32[32]{0:T(128)} %param.10) | copy-start | bytes 388
  13.8 31.2 %all-to-all-start = ((s32[64,1,2]{2,1,0:T(1,128)}), s32[64,1,2]{2,1,0:T(1,128)S(1)}, u32[]{:S(2)}, u32[]{:S(2)}) async-start(s32[64,1,2]{2,1,0:T(1,128)} %copy.15), calls=%async_computation | async-start | bytes 65536 | tf_op jit(solution)/shard_map/all_to_all | solution.py:74
  25.9 36.2 %collective-permute-start.1 = (f32[1,32,1024]{2,0,1:T(1,128)S(1)}, f32[1,32,1024]{2,0,1:T(1,128)S(1)}, u32[]{:S(2)}, u32[]{:S(2)}) collective-permute-start(f32[1,32,1024]{2,0,1:T(1,128)S(1)} %copy.19), channel_id=1, source_target_pairs={{4,0},{8,4},{12,8},{16,12},{20,16},{24,20},{28,24},{32,28},{36,32}... | collective-permute-start | bytes 393224 | tf_op jit(solution)/shard_map/ppermute | solution.py:19
  28.3 33.8 %collective-permute-start = (f32[1,32,1024]{2,0,1:T(1,128)S(1)}, f32[1,32,1024]{2,0,1:T(1,128)S(1)}, u32[]{:S(2)}, u32[]{:S(2)}) collective-permute-start(f32[1,32,1024]{2,0,1:T(1,128)S(1)} %copy.17), channel_id=1, source_target_pairs={{0,4},{4,8},{8,12},{12,16},{16,20},{20,24},{24,28},{28,32},{32,36}... | collective-permute-start | bytes 393224 | tf_op jit(solution)/shard_map/ppermute | solution.py:18
  45.0 36.1 %all-to-all-start.1 = ((bf16[64,2,32,128]{3,2,1,0:T(8,128)(2,1)}), bf16[64,2,32,128]{3,2,1,0:T(8,128)(2,1)S(1)}, u32[]{:S(2)}, u32[]{:S(2)}) async-start(bf16[64,2,32,128]{3,2,1,0:T(8,128)(2,1)} %scatter_fusion.1), calls=%async_computation.1 | async-start | bytes 2097152 | tf_op jit(solution)/shard_map/all_to_all | solution.py:73
  53.6 213.9 %all-gather.3.cloned.1.call-start = ((), (), s32[]{:S(2)}) async-start(), calls=%async_computation.2 | async-start | bytes 20971520 | tf_op jit(solution)/shard_map/all_gather | solution.py:81
  277.9 18.0 %copy-start = (f32[32,32,1024]{2,0,1:T(8,128)S(1)}, f32[32,32,1024]{2,0,1:T(8,128)}, u32[]{:S(2)}) copy-start(f32[32,32,1024]{2,0,1:T(8,128)} %reduce_sum.22) | copy-start | bytes 12582916
  277.9 18.0 %copy-start.1 = (f32[32,32,1024]{2,1,0:T(8,128)S(1)}, f32[32,32,1024]{2,1,0:T(8,128)}, u32[]{:S(2)}) copy-start(f32[32,32,1024]{2,1,0:T(8,128)} %param.8) | copy-start | bytes 12582916
  281.2 7.0 %collective-permute-start.2 = (f32[1,32,1024]{2,0,1:T(1,128)S(1)}, f32[1,32,1024]{2,0,1:T(1,128)S(1)}, u32[]{:S(2)}, u32[]{:S(2)}) collective-permute-start(f32[1,32,1024]{2,0,1:T(1,128)S(1)} %get-tuple-element.5), channel_id=1, source_target_pairs={{0,4},{4,8},{8,12},{12,16},{16,20},{20,24},{24,28},{28,32},{32,36}... | collective-permute-start | bytes 393224 | tf_op jit(solution)/shard_map/ppermute | solution.py:18
  286.3 9.6 %collective-permute-start.3 = (f32[1,32,1024]{2,0,1:T(1,128)S(1)}, f32[1,32,1024]{2,0,1:T(1,128)S(1)}, u32[]{:S(2)}, u32[]{:S(2)}) collective-permute-start(f32[1,32,1024]{2,0,1:T(1,128)S(1)} %get-tuple-element.6), channel_id=1, source_target_pairs={{4,0},{8,4},{12,8},{16,12},{20,16},{24,20},{28,24},{32,28},{36,32}... | collective-permute-start | bytes 393224 | tf_op jit(solution)/shard_map/ppermute | solution.py:19
Sparse Core Ops, SparseCore 0:
  110.0 157.4 all-gather.2
